TPU v7x, 32 devices: a whole 2x2x4 slice. The times are simulated.
32 devices in a mesh: eta: 2 (over x), phi: 4 (over z), replica: 4 (over y, core).
Axes of the slice: x: 2, y: 2, z: 4, core: 2. Of those that a mesh axis runs over, the one named last changes fastest.
Arguments:
- tokens: bfloat16 [4, 64, 128, 768], P('replica', 'eta', 'phi'), may hold values from -6 to 6
- send_pos: int32 [4, 2, 4, 8, 35], P('replica', 'eta', 'phi'), may hold values from 0 to 1024, as said below
- enc_src: int32 [4, 2, 4, 256], P('replica', 'eta', 'phi'), may hold values from 0 to 279, as said below
- window_id: int32 [4, 2, 4, 256], P('replica', 'eta', 'phi'), may hold values from 0 to 3
- enc_cot: bfloat16 [4, 2, 4, 256, 768], P('replica', 'eta', 'phi'), may hold values from -0.0625 to 0.0625
- w_qkv: bfloat16 [768, 2304], replicated, may hold values from -0.21875 to 0.21875
- head_scale: float32 [12], replicated, may hold values from 2 to 12
- w_out: bfloat16 [768, 768], replicated, may hold values from -0.21875 to 0.21875
- w_dec_in: bfloat16 [768, 384], replicated, may hold values from -0.21875 to 0.21875
- mask_token: bfloat16 [384], replicated, may hold values from -4 to 4
- conv_kernel: float32 [7, 7, 384], replicated, may hold values from -0.875 to 0.875
- w_up: bfloat16 [384, 768], replicated, may hold values from -0.3125 to 0.3125
- w_down: bfloat16 [768, 384], replicated, may hold values from -0.21875 to 0.21875
- w_head: bfloat16 [384, 128], replicated, may hold values from -0.3125 to 0.3125
Outputs:
- weight_grads: float32 [3072, 768], P(('eta', 'phi'))
- reconstruction: float32 [4, 64, 128, 128], P('replica', 'eta', 'phi')
Inputs may be any that keep to these rules, and one draw needn't show every extreme that they name: send_pos[e,a,b,d,k] is the cell of the k-th visible token that tile (a,b) sends to encoder shard d; 1024 marks an empty slot and empty slots follow the live ones. The visible cells of a tile are whole aligned 2 x 2 blocks, each sent exactly once; every encoder shard receives exactly 256 live slots; some tile fills all 35 slots to some shard. enc_src[e,a,b,r] = s * 35 + k names a live slot (send_pos of tile s towards this shard, slot k); each live slot arriving at the shard appears exactly once.
All inputs are finite; a program needn't handle non-finite values.
Results may differ from a plain program's by a relative error of at most 0.0095.
Values may be sent and summed in bfloat16 or wider, within the bound.
No kernel may reach another device: no remote copies, remote signals or barrier semaphores. Data moves between devices by JAX's collectives and lax.ppermute only.
A program may use at most 128 MiB of HBM per device.

v0:
```python
import jax
import jax.numpy as jnp
from jax import lax
from jax.sharding import PartitionSpec as P

norm_eps = 1e-05
length_eps = 1e-06
highest = lax.Precision.HIGHEST


def extended(block, sides, width):
    for axis, dim in sides:
        count = lax.axis_size(axis)
        forward = [(i, i + 1) for i in range(count - 1)]
        forward.append((count - 1, 0))
        backward = [(target, source) for source, target in forward]
        low = lax.ppermute(
            lax.slice_in_dim(block, block.shape[dim] - width, None, axis=dim), axis, forward
        )
        high = lax.ppermute(lax.slice_in_dim(block, 0, width, axis=dim), axis, backward)
        block = jnp.concatenate([low, block, high], axis=dim)
    return block


def plain_norm(values):
    centre = jnp.mean(values, axis=-1, keepdims=True)
    centred = values - centre
    spread = jnp.mean(centred * centred, axis=-1, keepdims=True)
    return centred * lax.rsqrt(spread + norm_eps)


def encoder_pass(enc_in, window, cotangent, w_qkv, head_scale, w_out):
    row_count, feature_width = enc_in.shape
    head_count = head_scale.shape[0]
    head_size = feature_width // head_count
    normed = plain_norm(enc_in.astype(jnp.float32)).astype(jnp.bfloat16)
    qkv = jnp.dot(normed, w_qkv, preferred_element_type=jnp.float32).reshape(
        row_count, 3, head_count, head_size
    )
    query = qkv[:, 0]
    keyed = qkv[:, 1]
    value_low = qkv[:, 2].astype(jnp.bfloat16)
    query_len = jnp.sqrt(jnp.sum(query * query, axis=-1, keepdims=True) + length_eps)
    key_len = jnp.sqrt(jnp.sum(keyed * keyed, axis=-1, keepdims=True) + length_eps)
    query_unit = query / query_len
    key_unit = keyed / key_len
    same_window = window[:, None] == window[None, :]
    scores = (
        jnp.einsum("qhd,khd->hqk", query_unit, key_unit, precision=highest)
        * head_scale[:, None, None]
    )
    raised = jnp.where(same_window[None], jnp.exp(scores), jnp.zeros((), jnp.float32))
    softmax_weights = raised / jnp.sum(raised, axis=-1, keepdims=True)
    softmax_low = softmax_weights.astype(jnp.bfloat16)
    attended = jnp.einsum(
        "hqk,khd->qhd", softmax_low, value_low, preferred_element_type=jnp.float32
    )
    attended = attended.reshape(row_count, feature_width).astype(jnp.bfloat16)
    enc_out = (
        enc_in.astype(jnp.float32) + jnp.dot(attended, w_out, preferred_element_type=jnp.float32)
    ).astype(jnp.bfloat16)
    grad_attended = lax.dot_general(
        cotangent, w_out, (((1,), (1,)), ((), ())), preferred_element_type=jnp.float32
    )
    grad_attended = grad_attended.astype(jnp.bfloat16).reshape(row_count, head_count, head_size)
    grad_soft = jnp.einsum(
        "qhd,khd->hqk", grad_attended, value_low, preferred_element_type=jnp.float32
    )
    grad_value = jnp.einsum(
        "hqk,qhd->khd", softmax_low, grad_attended, preferred_element_type=jnp.float32
    )
    grad_scores = softmax_weights * (
        grad_soft - jnp.sum(softmax_weights * grad_soft, axis=-1, keepdims=True)
    )
    grad_scores = grad_scores * head_scale[:, None, None]
    grad_qunit = jnp.einsum("hqk,khd->qhd", grad_scores, key_unit, precision=highest)
    grad_kunit = jnp.einsum("hqk,qhd->khd", grad_scores, query_unit, precision=highest)
    grad_query = (
        grad_qunit - query_unit * jnp.sum(query_unit * grad_qunit, axis=-1, keepdims=True)
    ) / query_len
    grad_key = (
        grad_kunit - key_unit * jnp.sum(key_unit * grad_kunit, axis=-1, keepdims=True)
    ) / key_len
    grad_qkv = (
        jnp.stack([grad_query, grad_key, grad_value], axis=1)
        .reshape(row_count, 3 * feature_width)
        .astype(jnp.bfloat16)
    )
    contract_rows = (((0,), (0,)), ((), ()))
    term = jnp.concatenate(
        [
            lax.dot_general(grad_qkv, normed, contract_rows, preferred_element_type=jnp.float32),
            lax.dot_general(cotangent, attended, contract_rows, preferred_element_type=jnp.float32),
        ],
        axis=0,
    )
    return (enc_out, term)


def body(
    tokens,
    send_pos,
    enc_src,
    window_id,
    enc_cot,
    w_qkv,
    head_scale,
    w_out,
    w_dec_in,
    mask_token,
    conv_kernel,
    w_up,
    w_down,
    w_head,
):
    eta_cells = tokens.shape[1]
    phi_cells = tokens.shape[2]
    feature_width = tokens.shape[3]
    dec_width = w_dec_in.shape[1]
    tile_len = eta_cells * phi_cells
    eta_count = lax.axis_size("eta")
    phi_count = lax.axis_size("phi")
    group_size = eta_count * phi_count
    slot_count = send_pos.shape[-1]
    flat_tile = tokens.reshape(tile_len, feature_width)
    slot_cells = send_pos.reshape(group_size * slot_count)
    outgoing = jnp.take(flat_tile, jnp.minimum(slot_cells, tile_len - 1), axis=0)
    outgoing = outgoing.reshape(group_size, slot_count, feature_width)
    arrived = lax.all_to_all(outgoing, ("eta", "phi"), split_axis=0, concat_axis=0, tiled=True)
    arrived = arrived.reshape(group_size * slot_count, feature_width)
    sources = enc_src.reshape(-1)
    enc_in = jnp.take(arrived, sources, axis=0)
    enc_out, term = encoder_pass(
        enc_in, window_id.reshape(-1), enc_cot.reshape(-1, feature_width), w_qkv, head_scale, w_out
    )
    grad_share = lax.psum_scatter(term, ("eta", "phi", "replica"), scatter_dimension=0, tiled=True)
    grad_total = lax.all_gather(
        grad_share.astype(jnp.bfloat16), "replica", axis=0, tiled=True
    ).astype(grad_share.dtype)
    outbound = (
        jnp.zeros((group_size * slot_count, feature_width), jnp.bfloat16).at[sources].set(enc_out)
    )
    returned = lax.all_to_all(
        outbound.reshape(group_size, slot_count, feature_width),
        ("eta", "phi"),
        split_axis=0,
        concat_axis=0,
        tiled=True,
    )
    returned = returned.reshape(group_size * slot_count, feature_width)
    dec_slots = jnp.dot(returned, w_dec_in, preferred_element_type=jnp.float32).astype(jnp.bfloat16)
    filled = (
        jnp.zeros((tile_len, dec_width), jnp.bfloat16).at[slot_cells].set(dec_slots, mode="drop")
    )
    seen_cells = jnp.zeros((tile_len,), jnp.bool_).at[slot_cells].set(True, mode="drop")
    dec_grid = jnp.where(seen_cells[:, None], filled, mask_token).reshape(
        eta_cells, phi_cells, dec_width
    )
    kernel_span = conv_kernel.shape[0]
    rim_width = kernel_span // 2
    padded = extended(dec_grid, (("eta", 0), ("phi", 1)), rim_width)
    eta_place = lax.axis_index("eta")
    rim_line = lax.broadcasted_iota(jnp.int32, (eta_cells + 2 * rim_width, 1, 1), 0)
    keep_rim = jnp.logical_and(
        jnp.logical_or(rim_line >= rim_width, eta_place > 0),
        jnp.logical_or(rim_line < eta_cells + rim_width, eta_place < eta_count - 1),
    )
    padded = jnp.where(keep_rim, padded, jnp.zeros((), padded.dtype))
    mixed_cells = jnp.zeros((eta_cells, phi_cells, dec_width), jnp.float32)
    for row_shift in range(kernel_span):
        for col_shift in range(kernel_span):
            window_cells = padded[
                row_shift : row_shift + eta_cells, col_shift : col_shift + phi_cells
            ].astype(jnp.float32)
            mixed_cells = mixed_cells + conv_kernel[row_shift, col_shift] * window_cells
    dec_normed = plain_norm(mixed_cells).astype(jnp.bfloat16).reshape(tile_len, dec_width)
    hidden = jax.nn.gelu(
        jnp.dot(dec_normed, w_up, preferred_element_type=jnp.float32), approximate=False
    ).astype(jnp.bfloat16)
    decoded = (
        dec_grid.reshape(tile_len, dec_width).astype(jnp.float32)
        + jnp.dot(hidden, w_down, preferred_element_type=jnp.float32)
    ).astype(jnp.bfloat16)
    reconstruction = jnp.dot(decoded, w_head, preferred_element_type=jnp.float32).reshape(
        1, eta_cells, phi_cells, -1
    )
    return (grad_total, reconstruction)


def solution(mesh):
    in_specs = (
        P("replica", "eta", "phi", None),
        P("replica", "eta", "phi", None, None),
        P("replica", "eta", "phi", None),
        P("replica", "eta", "phi", None),
        P("replica", "eta", "phi", None, None),
        P(),
        P(),
        P(),
        P(),
        P(),
        P(),
        P(),
        P(),
        P(),
    )
    out_specs = (P(("eta", "phi"), None), P("replica", "eta", "phi", None))
    return jax.shard_map(body, mesh=mesh, in_specs=in_specs, out_specs=out_specs, check_vma=False)
```

profile of v0, /device:TPU:0, one launch (start us, length us, event | category | flops | bytes accessed | tf_op | source)
XLA Modules:
  0.0 229.6 jit_solution(4999208129221974570)
XLA Ops:
  9.6 4.6 %gather_fusion = bf16[280,768]{1,0:T(8,128)(2,1)} fusion(bf16[1024,768]{1,0:T(8,128)(2,1)} %bitcast.105, s32[1024]{0:T(1024)S(1)} %pad_clamp_fusion.1), kind=kCustom, calls=%fused_computation | custom fusion | bytes 861280 | tf_op jit(solution)/shard_map/jit(_take)/gather | solution.py:127
  14.1 1.9 gather.11
  16.1 1.9 broadcast_select_fusion.1
  18.0 7.3 %all-to-all-start = ((bf16[8,35,768]{2,1,0:T(8,128)(2,1)}), bf16[8,35,768]{2,1,0:T(8,128)(2,1)}, u32[]{:S(2)}, u32[]{:S(2)}) async-start(bf16[8,35,768]{2,1,0:T(8,128)(2,1)} %broadcast_select_fusion.1), calls=%async_computation | async-start | bytes 983040 | tf_op jit(solution)/shard_map/all_to_all | solution.py:129
  25.3 2.6 %convolution_convert_fusion.2 = bf16[256,768]{1,0:T(8,128)(2,1)} fusion(bf16[768,768]{1,0:T(8,128)(2,1)} %param.21, bf16[1,1,1,256,768]{4,3,2,1,0:T(8,128)(2,1)} %param.18), kind=kOutput, calls=%fused_computation.52 | convolution fusion | flops 302186496 | bytes 1966080 | tf_op jit(solution)/shard_map/dot_general | solution.py:62
  28.0 1.9 copy.32
  31.3 8.7 %all-to-all-done = bf16[8,35,768]{2,1,0:T(8,128)(2,1)} async-done(((bf16[8,35,768]{2,1,0:T(8,128)(2,1)}), bf16[8,35,768]{2,1,0:T(8,128)(2,1)}, u32[]{:S(2)}, u32[]{:S(2)}) %all-to-all-start) | async-done | bytes 430112 | tf_op jit(solution)/shard_map/all_to_all | solution.py:129
  40.0 1.9 reshape.239
  42.0 3.2 %gather_fusion.1 = bf16[256,768]{1,0:T(8,128)(2,1)} fusion(bf16[280,768]{1,0:T(8,128)(2,1)} %reshape.239, s32[1024]{0:T(1024)S(1)} %pad_clamp_fusion), kind=kCustom, calls=%fused_computation.1 | custom fusion | bytes 787456 | tf_op jit(solution)/shard_map/jit(_take)/gather | solution.py:132
  47.7 2.6 %fusion.53 = f32[256,2304]{0,1:T(8,128)S(1)} fusion(bf16[768,2304]{1,0:T(8,128)(2,1)S(1)} %copy-done, f32[256]{0:T(256)S(1)} %add_rsqrt_fusion.1, f32[256]{0:T(256)S(1)} %broadcast_multiply_fusion.1, bf16[256,768]{1,0:T(8,128)(2,1)} %gather_fusion.1, pred[256]{0:T(512)(128)(4,1)S(1)} %compare_and_fusion.1), kind=kOutput, calls=%fused_computation.163 | convolution fusion | flops 906952704 | bytes 6293760 | tf_op jit(solution)/shard_map/dot_general | solution.py:37
  51.2 3.4 %fusion.13 = (f32[12,256]{1,0:T(8,128)S(1)}, f32[12,256,256]{1,2,0:T(8,128)S(1)}) fusion(f32[12]{0:T(128)S(1)} %copy-done.44, pred[256,256]{0,1:T(8,128)(4,1)S(1)} %copy-done.6, f32[256,3,12,64]{0,3,2,1:T(8,128)S(1)} %bitcast.107, f32[256,12]{0,1:T(8,128)S(1)} %get-tuple-element.66, f32[256,12]{0,1:T(8,128)S(1)} %get-tuple-element.65), kind=kOutput, calls=%fused_computation.31 | convolution fusion | flops 606729216 | bytes 4829696 | tf_op jit(solution)/shard_map/qhd,khd->hqk/dot_general | solution.py:49
  57.6 4.1 %convolution_bitcast_fusion.1 = f32[256,12,64]{0,2,1:T(8,128)S(1)} fusion(f32[12,256,256]{1,2,0:T(8,128)S(1)} %get-tuple-element.64, f32[12,256]{1,0:T(8,128)S(1)} %get-tuple-element.63, f32[12]{0:T(128)S(1)} %copy-done.44, f32[256,3,12,64]{0,3,2,1:T(8,128)S(1)} %bitcast.110, f32[256,12]{0,1:T(8,128)S(1)} %get-tuple-element.65, ...), kind=kOutput, calls=%fused_computation.44 | convolution fusion | flops 608894976 | bytes 7979520 | tf_op jit(solution)/shard_map/hqk,qhd->khd/dot_general | solution.py:77
  61.7 3.1 %convolution_bitcast_fusion.2 = f32[256,12,64]{0,2,1:T(8,128)S(1)} fusion(f32[12,256,256]{1,2,0:T(8,128)S(1)} %get-tuple-element.64, f32[12,256]{1,0:T(8,128)S(1)} %get-tuple-element.63, f32[12]{0:T(128)S(1)} %copy-done.44, f32[256,3,12,64]{0,3,2,1:T(8,128)S(1)} %bitcast.111, f32[256,12]{0,1:T(8,128)S(1)} %get-tuple-element.66, ...), kind=kOutput, calls=%fused_computation.45 | convolution fusion | flops 608894976 | bytes 7979520 | tf_op jit(solution)/shard_map/hqk,khd->qhd/dot_general | solution.py:76
  64.8 1.9 convolution_bitcast_fusion
  68.3 4.1 %fusion.51 = f32[2304,768]{1,0:T(8,128)} fusion(bf16[256,2304]{0,1:T(8,128)(2,1)S(1)} %bitcast.104, f32[256]{0:T(256)S(1)} %add_rsqrt_fusion.1, f32[256]{0:T(256)S(1)} %broadcast_multiply_fusion.1, bf16[256,768]{1,0:T(8,128)(2,1)S(1)} %copy-done.1, pred[256]{0:T(512)(128)(4,1)S(1)} %compare_and_fusion.1), kind=kOutput, calls=%fused_computation.162 | convolution fusion | flops 906952704 | bytes 8653056 | tf_op jit(solution)/shard_map/dot_general | solution.py:92
  72.4 8.0 %pad_maximum_fusion = f32[3072,768]{1,0:T(8,128)} fusion(f32[768,768]{1,0:T(8,128)} %convolution_bitcast_fusion, f32[2304,768]{1,0:T(8,128)} %fusion.51), kind=kLoop, calls=%fused_computation.7 | loop fusion | flops 2359296 | bytes 18874368 | tf_op jit(solution)/shard_map/concatenate | solution.py:90
  80.3 2.7 %fusion.21 = bf16[256,768]{1,0:T(8,128)(2,1)} fusion(bf16[256,768]{0,1:T(8,128)(2,1)} %bitcast.116, bf16[768,768]{1,0:T(8,128)(2,1)} %param.21, bf16[256,768]{1,0:T(8,128)(2,1)} %gather_fusion.1, pred[256]{0:T(512)(128)(4,1)S(1)} %compare_and_fusion.1), kind=kOutput, calls=%fused_computation.47 | convolution fusion | flops 302776320 | bytes 2359552 | tf_op jit(solution)/shard_map/dot_general | solution.py:60
  83.1 2.8 %scatter_custom_fusion.1 = bf16[280,768]{1,0:T(8,128)(2,1)} fusion(s32[256]{0:T(256)S(1)} %bitcast.123, bf16[256,768]{1,0:T(8,128)(2,1)} %fusion.21, bf16[]{:T(256)} %constant.20.clone.1), kind=kCustom, calls=%fused_computation.86 | custom fusion | bytes 430592 | tf_op jit(solution)/shard_map/scatter | solution.py:141
  85.9 1.9 reshape.244
  87.8 4.1 %all-to-all-start.1 = ((bf16[8,35,768]{2,1,0:T(8,128)(2,1)}), bf16[8,35,768]{2,1,0:T(8,128)(2,1)}, u32[]{:S(2)}, u32[]{:S(2)}) async-start(bf16[8,35,768]{2,1,0:T(8,128)(2,1)} %reshape.244), calls=%async_computation.2 | async-start | bytes 983040 | tf_op jit(solution)/shard_map/all_to_all | solution.py:143
  92.0 2.3 scatter_custom_fusion
  98.1 7.4 %all-to-all-done.1 = bf16[8,35,768]{2,1,0:T(8,128)(2,1)} async-done(((bf16[8,35,768]{2,1,0:T(8,128)(2,1)}), bf16[8,35,768]{2,1,0:T(8,128)(2,1)}, u32[]{:S(2)}, u32[]{:S(2)}) %all-to-all-start.1) | async-done | bytes 430112 | tf_op jit(solution)/shard_map/all_to_all | solution.py:143
  105.5 2.0 reshape.245
  107.5 2.3 %convolution_convert_fusion.3 = bf16[280,384]{1,0:T(8,128)(2,1)} fusion(bf16[280,768]{1,0:T(8,128)(2,1)} %reshape.245, bf16[768,384]{1,0:T(8,128)(2,1)} %param.22), kind=kOutput, calls=%fused_computation.56 | convolution fusion | flops 165258240 | bytes 1234944 | tf_op jit(solution)/shard_map/dot_general | solution.py:151
  109.8 2.9 %scatter_custom_fusion.2 = bf16[1024,384]{1,0:T(8,128)(2,1)} fusion(s32[280]{0:T(512)} %get-tuple-element.53, bf16[280,384]{1,0:T(8,128)(2,1)} %convolution_convert_fusion.3, bf16[]{:T(256)} %constant.20.clone.1), kind=kCustom, calls=%fused_computation.83 | custom fusion | bytes 786944 | tf_op jit(solution)/shard_map/scatter | solution.py:153
  119.9 3.8 %collective-permute-start.3 = (bf16[38,3,384]{2,1,0:T(4,128)(2,1)S(1)}, bf16[38,3,384]{2,1,0:T(4,128)(2,1)S(1)}, u32[]{:S(2)}, u32[]{:S(2)}) collective-permute-start(bf16[38,3,384]{2,1,0:T(4,128)(2,1)S(1)} %get-tuple-element.58), channel_id=1, source_target_pairs={{4,0},{8,4},{12,8},{0,12},{5,1},{9,5},{13,9},{1,13},{6,2},{10,6},{... | collective-permute-start | bytes 262664 | tf_op jit(solution)/shard_map/ppermute | solution.py:20
  123.7 2.8 %collective-permute-done.2 = bf16[38,3,384]{2,1,0:T(4,128)(2,1)S(1)} collective-permute-done((bf16[38,3,384]{2,1,0:T(4,128)(2,1)S(1)}, bf16[38,3,384]{2,1,0:T(4,128)(2,1)S(1)}, u32[]{:S(2)}, u32[]{:S(2)}) %collective-permute-start.2) | collective-permute-done | bytes 87584 | tf_op jit(solution)/shard_map/ppermute | solution.py:17
  127.3 11.6 %fusion.66 = (f32[32,32]{1,0:T(8,128)S(1)}, f32[32,32,384]{2,1,0:T(8,128)S(1)}) fusion(bf16[38,38,384]{2,1,0:T(8,128)(2,1)S(1)} %maximum_select_fusion, f32[384]{0:T(512)S(1)} %get-tuple-element.51, f32[384]{0:T(512)S(1)} %get-tuple-element.52, f32[384]{0:T(512)S(1)} %get-tuple-element.5, f32[384]{0:T(512)S(1)} %get-tuple-element.6, ...), kind=kLoop, calls=%fused_computation.165 | loop fusion | flops 57801728 | bytes 40187392 | tf_op jit(solution)/shard_map/reduce_sum | solution.py:26
  140.4 8.7 %fusion.4 = bf16[1024,768]{1,0:T(8,128)(2,1)} fusion(bf16[1024,384]{1,0:T(8,128)(2,1)S(1)} %bitcast.114, bf16[384,768]{1,0:T(8,128)(2,1)S(1)} %copy-done.43), kind=kOutput, calls=%fused_computation.11 | convolution fusion | flops 655097856 | bytes 2949120 | tf_op jit(solution)/shard_map/dot_general | solution.py:178
  149.1 3.8 %fusion.20 = f32[1024,128]{1,0:T(8,128)} fusion(bf16[384,128]{1,0:T(8,128)(2,1)} %param.27, bf16[1024,384]{1,0:T(8,128)(2,1)} %copy-done.2, bf16[1024,768]{1,0:T(8,128)(2,1)} %fusion.4, bf16[768,384]{1,0:T(8,128)(2,1)} %param.26), kind=kOutput, calls=%fused_computation.46 | convolution fusion | flops 705822720 | bytes 3571712 | tf_op jit(solution)/shard_map/dot_general | solution.py:184
  152.9 60.6 %reduce-scatter.2.cloned.1.call-done = f32[96,768]{1,0:T(8,128)} async-done(((f32[3072,768]{1,0:T(8,128)}), f32[96,768]{1,0:T(8,128)}) %reduce-scatter.2.cloned.1.call-update) | async-done | bytes 294928 | tf_op jit(solution)/shard_map/reduce_scatter | solution.py:136
  214.4 7.2 %all_gather.3 = bf16[384,768]{1,0:T(8,128)(2,1)S(1)} all-gather(bf16[96,768]{1,0:T(8,128)(2,1)S(1)} %convert_element_type.212), channel_id=1, replica_groups=mesh['eta'=2,'phi'=4,'replica'=4] {'replica'}, dimensions={0}, use_global_device_ids=true | all-gather | bytes 737280 | tf_op jit(solution)/shard_map/all_gather | solution.py:137
  (133 shorter events, 26.4 us)
Async XLA Ops:
  7.2 40.5 %copy-start = (bf16[768,2304]{1,0:T(8,128)(2,1)S(1)}, bf16[768,2304]{1,0:T(8,128)(2,1)}, u32[]{:S(2)}) copy-start(bf16[768,2304]{1,0:T(8,128)(2,1)} %param.19) | copy-start | bytes 10616836
  18.0 22.0 %all-to-all-start = ((bf16[8,35,768]{2,1,0:T(8,128)(2,1)}), bf16[8,35,768]{2,1,0:T(8,128)(2,1)}, u32[]{:S(2)}, u32[]{:S(2)}) async-start(bf16[8,35,768]{2,1,0:T(8,128)(2,1)} %broadcast_select_fusion.1), calls=%async_computation | async-start | bytes 983040 | tf_op jit(solution)/shard_map/all_to_all | solution.py:129
  25.3 188.2 %reduce-scatter.2.cloned.1.call-start = ((), (), s32[]{:S(2)}) async-start(), calls=%async_computation.3 | async-start | bytes 9732096 | tf_op jit(solution)/shard_map/reduce_scatter | solution.py:136
  55.4 9.4 %copy-start.4 = (bf16[12,64,256]{2,1,0:T(8,128)(2,1)}, bf16[12,64,256]{2,1,0:T(8,128)(2,1)S(1)}, u32[]{:S(2)}) copy-start(bf16[12,64,256]{2,1,0:T(8,128)(2,1)S(1)} %convolution_convert_fusion) | copy-start | bytes 1179652
  87.8 17.7 %all-to-all-start.1 = ((bf16[8,35,768]{2,1,0:T(8,128)(2,1)}), bf16[8,35,768]{2,1,0:T(8,128)(2,1)}, u32[]{:S(2)}, u32[]{:S(2)}) async-start(bf16[8,35,768]{2,1,0:T(8,128)(2,1)} %reshape.244), calls=%async_computation.2 | async-start | bytes 983040 | tf_op jit(solution)/shard_map/all_to_all | solution.py:143
  114.2 12.8 %copy-start.2 = (bf16[1024,384]{1,0:T(8,128)(2,1)}, bf16[1024,384]{1,0:T(8,128)(2,1)S(1)}, u32[]{:S(2)}) copy-start(bf16[1024,384]{1,0:T(8,128)(2,1)S(1)} %broadcast_select_fusion) | copy-start | bytes 2359300
  114.2 4.4 %collective-permute-start.1 = (bf16[3,32,384]{2,1,0:T(8,128)(2,1)S(1)}, bf16[3,32,384]{2,1,0:T(8,128)(2,1)S(1)}, u32[]{:S(2)}, u32[]{:S(2)}) collective-permute-start(bf16[3,32,384]{2,1,0:T(8,128)(2,1)S(1)} %bitcast.120), channel_id=1, source_target_pairs={{16,0},{0,16},{17,1},{1,17},{18,2},{2,18},{19,3},{3,19},{20,4},{4,... | collective-permute-start | bytes 221192 | tf_op jit(solution)/shard_map/ppermute | solution.py:20
  114.8 4.6 %collective-permute-start = (bf16[3,32,384]{2,1,0:T(8,128)(2,1)S(1)}, bf16[3,32,384]{2,1,0:T(8,128)(2,1)S(1)}, u32[]{:S(2)}, u32[]{:S(2)}) collective-permute-start(bf16[3,32,384]{2,1,0:T(8,128)(2,1)S(1)} %bitcast.119), channel_id=1, source_target_pairs={{0,16},{16,0},{1,17},{17,1},{2,18},{18,2},{3,19},{19,3},{4,20},{20... | collective-permute-start | bytes 221192 | tf_op jit(solution)/shard_map/ppermute | solution.py:17
  119.4 7.6 %copy-start.11 = (f32[384]{0:T(512)S(1)}, f32[384]{0:T(512)}, u32[]{:S(2)}) copy-start(f32[384]{0:T(512)} %get-tuple-element.12) | copy-start | bytes 4612
  119.4 7.6 %copy-start.12 = (f32[384]{0:T(512)S(1)}, f32[384]{0:T(512)}, u32[]{:S(2)}) copy-start(f32[384]{0:T(512)} %get-tuple-element.13) | copy-start | bytes 4612
  119.4 7.6 %copy-start.13 = (f32[384]{0:T(512)S(1)}, f32[384]{0:T(512)}, u32[]{:S(2)}) copy-start(f32[384]{0:T(512)} %get-tuple-element.14) | copy-start | bytes 4612
  119.4 7.6 %copy-start.14 = (f32[384]{0:T(512)S(1)}, f32[384]{0:T(512)}, u32[]{:S(2)}) copy-start(f32[384]{0:T(512)} %get-tuple-element.15) | copy-start | bytes 4612
  119.5 7.6 %copy-start.15 = (f32[384]{0:T(512)S(1)}, f32[384]{0:T(512)}, u32[]{:S(2)}) copy-start(f32[384]{0:T(512)} %get-tuple-element.16) | copy-start | bytes 4612
  119.5 7.6 %copy-start.16 = (f32[384]{0:T(512)S(1)}, f32[384]{0:T(512)}, u32[]{:S(2)}) copy-start(f32[384]{0:T(512)} %get-tuple-element.17) | copy-start | bytes 4612
  119.5 7.6 %copy-start.17 = (f32[384]{0:T(512)S(1)}, f32[384]{0:T(512)}, u32[]{:S(2)}) copy-start(f32[384]{0:T(512)} %get-tuple-element.18) | copy-start | bytes 4612
  119.5 7.6 %copy-start.18 = (f32[384]{0:T(512)S(1)}, f32[384]{0:T(512)}, u32[]{:S(2)}) copy-start(f32[384]{0:T(512)} %get-tuple-element.19) | copy-start | bytes 4612
  119.5 7.6 %copy-start.19 = (f32[384]{0:T(512)S(1)}, f32[384]{0:T(512)}, u32[]{:S(2)}) copy-start(f32[384]{0:T(512)} %get-tuple-element.20) | copy-start | bytes 4612
  119.5 7.6 %copy-start.20 = (f32[384]{0:T(512)S(1)}, f32[384]{0:T(512)}, u32[]{:S(2)}) copy-start(f32[384]{0:T(512)} %get-tuple-element.21) | copy-start | bytes 4612
  119.5 7.6 %copy-start.21 = (f32[384]{0:T(512)S(1)}, f32[384]{0:T(512)}, u32[]{:S(2)}) copy-start(f32[384]{0:T(512)} %get-tuple-element.22) | copy-start | bytes 4612
  119.5 7.6 %copy-start.22 = (f32[384]{0:T(512)S(1)}, f32[384]{0:T(512)}, u32[]{:S(2)}) copy-start(f32[384]{0:T(512)} %get-tuple-element.23) | copy-start | bytes 4612
  119.5 7.6 %copy-start.23 = (f32[384]{0:T(512)S(1)}, f32[384]{0:T(512)}, u32[]{:S(2)}) copy-start(f32[384]{0:T(512)} %get-tuple-element.24) | copy-start | bytes 4612
  119.5 7.6 %copy-start.24 = (f32[384]{0:T(512)S(1)}, f32[384]{0:T(512)}, u32[]{:S(2)}) copy-start(f32[384]{0:T(512)} %get-tuple-element.25) | copy-start | bytes 4612
  119.6 7.6 %copy-start.25 = (f32[384]{0:T(512)S(1)}, f32[384]{0:T(512)}, u32[]{:S(2)}) copy-start(f32[384]{0:T(512)} %get-tuple-element.26) | copy-start | bytes 4612
  119.6 7.6 %copy-start.26 = (f32[384]{0:T(512)S(1)}, f32[384]{0:T(512)}, u32[]{:S(2)}) copy-start(f32[384]{0:T(512)} %get-tuple-element.27) | copy-start | bytes 4612
  119.6 7.6 %copy-start.27 = (f32[384]{0:T(512)S(1)}, f32[384]{0:T(512)}, u32[]{:S(2)}) copy-start(f32[384]{0:T(512)} %get-tuple-element.28) | copy-start | bytes 4612
  119.6 7.6 %copy-start.28 = (f32[384]{0:T(512)S(1)}, f32[384]{0:T(512)}, u32[]{:S(2)}) copy-start(f32[384]{0:T(512)} %get-tuple-element.29) | copy-start | bytes 4612
  119.6 7.6 %copy-start.29 = (f32[384]{0:T(512)S(1)}, f32[384]{0:T(512)}, u32[]{:S(2)}) copy-start(f32[384]{0:T(512)} %get-tuple-element.30) | copy-start | bytes 4612
  119.6 7.6 %copy-start.30 = (f32[384]{0:T(512)S(1)}, f32[384]{0:T(512)}, u32[]{:S(2)}) copy-start(f32[384]{0:T(512)} %get-tuple-element.31) | copy-start | bytes 4612
  119.6 7.6 %copy-start.31 = (f32[384]{0:T(512)S(1)}, f32[384]{0:T(512)}, u32[]{:S(2)}) copy-start(f32[384]{0:T(512)} %get-tuple-element.32) | copy-start | bytes 4612
  119.6 7.6 %copy-start.32 = (f32[384]{0:T(512)S(1)}, f32[384]{0:T(512)}, u32[]{:S(2)}) copy-start(f32[384]{0:T(512)} %get-tuple-element.33) | copy-start | bytes 4612
  119.8 6.7 %collective-permute-start.2 = (bf16[38,3,384]{2,1,0:T(4,128)(2,1)S(1)}, bf16[38,3,384]{2,1,0:T(4,128)(2,1)S(1)}, u32[]{:S(2)}, u32[]{:S(2)}) collective-permute-start(bf16[38,3,384]{2,1,0:T(4,128)(2,1)S(1)} %get-tuple-element.57), channel_id=1, source_target_pairs={{0,4},{4,8},{8,12},{12,0},{1,5},{5,9},{9,13},{13,1},{2,6},{6,10},{... | collective-permute-start | bytes 262664 | tf_op jit(solution)/shard_map/ppermute | solution.py:17
  119.9 6.6 %collective-permute-start.3 = (bf16[38,3,384]{2,1,0:T(4,128)(2,1)S(1)}, bf16[38,3,384]{2,1,0:T(4,128)(2,1)S(1)}, u32[]{:S(2)}, u32[]{:S(2)}) collective-permute-start(bf16[38,3,384]{2,1,0:T(4,128)(2,1)S(1)} %get-tuple-element.58), channel_id=1, source_target_pairs={{4,0},{8,4},{12,8},{0,12},{5,1},{9,5},{13,9},{1,13},{6,2},{10,6},{... | collective-permute-start | bytes 262664 | tf_op jit(solution)/shard_map/ppermute | solution.py:20
  (20 other events, 109.0 us)
Sparse Core Ops, SparseCore 0:
  80.5 132.9 reduce-scatter.1
where the time goes:
time: 231 us; the launch traced here: 230 us
  waiting for transfers between devices  81.7 us (35%)
  matrix products  42.4 us (18%)
  local copies, waits for them, and re-layouts  33.7 us (15%)
  other arithmetic  32.4 us (14%)
  starting transfers between devices  17.4 us (8%)
  between operations  14.8 us (6%)
  blocking collectives  7.22 us (3%)
    reduce_scatter x1, waiting for transfers between devices, body(): lax.psum_scatter(term, ('eta', 'phi', 'replica'), scatter_dimension=0, ti...  60.6 us
    reduce_sum x2, other arithmetic, plain_norm(): centre = jnp.mean(values, axis=-1, keepdims=True)  12.8 us
    dot_general x1, matrix products, body(): jnp.dot(dec_normed, w_up, preferred_element_type=jnp.float32)  8.74 us
    all_to_all x1, waiting for transfers between devices, body(): lax.all_to_all(outgoing, ('eta', 'phi'), split_axis=0, concat_axis=0, til...  8.72 us
    concatenate x1, other arithmetic, encoder_pass(): jnp.concatenate([lax.dot_general(grad_qkv, normed, contract_rows, preferr...  7.96 us
    all_to_all x1, waiting for transfers between devices, body(): lax.all_to_all(outbound.reshape(group_size, slot_count, feature_width), (...  7.45 us
    all_to_all x1, starting transfers between devices, body(): lax.all_to_all(outgoing, ('eta', 'phi'), split_axis=0, concat_axis=0, til...  7.25 us
    all_gather x1, blocking collectives, body(): lax.all_gather(grad_share.astype(jnp.bfloat16), 'replica', axis=0, tiled=...  7.22 us
  transfers between devices with their start and end apart: 7, of which 6 were waited for; matrix products, arithmetic and copies ran while one was open for 24% of the time, Pallas kernels for 0%

commit v1 on v0

--- a/solution.py
+++ b/solution.py
@@ -134,9 +134,22 @@
         enc_in, window_id.reshape(-1), enc_cot.reshape(-1, feature_width), w_qkv, head_scale, w_out
     )
     grad_share = lax.psum_scatter(term, ("eta", "phi", "replica"), scatter_dimension=0, tiled=True)
-    grad_total = lax.all_gather(
-        grad_share.astype(jnp.bfloat16), "replica", axis=0, tiled=True
-    ).astype(grad_share.dtype)
+
+    def produce_tracks(buf):
+        group_axis = "replica"
+        carry_in, v1 = (lax.axis_size(group_axis), lax.axis_index(group_axis))
+        e_next, work_now = (buf, 1)
+        while work_now < carry_in:
+            left_arr = lax.ppermute(
+                e_next, group_axis, tuple(((i0, i0 ^ work_now) for i0 in range(carry_in)))
+            )
+            new = jnp.concatenate([e_next, left_arr], axis=0)
+            block_next = jnp.concatenate([left_arr, e_next], axis=0)
+            e_next = jnp.where(v1 & work_now == 0, new, block_next)
+            work_now = 2 * work_now
+        return e_next
+
+    grad_total = produce_tracks(grad_share.astype(jnp.bfloat16)).astype(grad_share.dtype)
     outbound = (
         jnp.zeros((group_size * slot_count, feature_width), jnp.bfloat16).at[sources].set(enc_out)
     )

time: 231 us -> 245 us (1.061)
  waiting for transfers between devices: 81.7 us -> 98.4 us
  blocking collectives: 7.22 us -> 0 us
  other arithmetic: 32.4 us -> 35.3 us
    reduce_scatter x1, waiting for transfers between devices: 60.6 us -> 72.8 us  [body(): lax.psum_scatter(term, ('eta', 'phi', 'replica'), scatter_dimension=0, ti...]
    all_gather x1 -> x0, blocking collectives: 7.22 us -> none  [body(): lax.all_gather(grad_share.astype(jnp.bfloat16), 'replica', axis=0, tiled=...]
    ppermute x0 -> x2, waiting for transfers between devices: none -> 4.45 us  [produce_tracks(): lax.ppermute(e_next, group_axis, tuple(((i0, i0 ^ work_now) for i0 in ran...]
  transfers between devices with their start and end apart: 7 -> 9, of which waited for: 6 -> 7; matrix products, arithmetic and copies ran while one was open for 24% -> 23% of each run, Pallas kernels for 0% -> 0%
where the time goes in v1:
time: 245 us; the launch traced here: 243 us
  waiting for transfers between devices  98.4 us (40%)
  matrix products  42.9 us (18%)
  other arithmetic  35.3 us (14%)
  local copies, waits for them, and re-layouts  32.9 us (13%)
  starting transfers between devices  18.9 us (8%)
  between operations  14.8 us (6%)
    reduce_scatter x1, waiting for transfers between devices, body(): lax.psum_scatter(term, ('eta', 'phi', 'replica'), scatter_dimension=0, ti...  72.8 us
    reduce_sum x2, other arithmetic, plain_norm(): centre = jnp.mean(values, axis=-1, keepdims=True)  12.8 us
    dot_general x1, matrix products, body(): jnp.dot(dec_normed, w_up, preferred_element_type=jnp.float32)  9.25 us
    all_to_all x1, waiting for transfers between devices, body(): lax.all_to_all(outgoing, ('eta', 'phi'), split_axis=0, concat_axis=0, til...  8.72 us
    concatenate x1, other arithmetic, encoder_pass(): jnp.concatenate([lax.dot_general(grad_qkv, normed, contract_rows, preferr...  7.96 us
    all_to_all x1, waiting for transfers between devices, body(): lax.all_to_all(outbound.reshape(group_size, slot_count, feature_width), (...  7.47 us
    all_to_all x1, starting transfers between devices, body(): lax.all_to_all(outgoing, ('eta', 'phi'), split_axis=0, concat_axis=0, til...  7.25 us
    gather x2, local copies, waits for them, and re-layouts, body(): jnp.take(flat_tile, jnp.minimum(slot_cells, tile_len - 1), axis=0)  6.49 us
  transfers between devices with their start and end apart: 9, of which 7 were waited for; matrix products, arithmetic and copies ran while one was open for 23% of the time, Pallas kernels for 0%

profile of v1, /device:TPU:0, one launch (start us, length us, event | category | flops | bytes accessed | tf_op | source)
XLA Modules:
  0.0 243.3 jit_solution(9482490867880476412)
XLA Ops:
  9.5 4.6 %gather_fusion = bf16[280,768]{1,0:T(8,128)(2,1)} fusion(bf16[1024,768]{1,0:T(8,128)(2,1)} %bitcast.102, s32[1024]{0:T(1024)S(1)} %pad_clamp_fusion.1), kind=kCustom, calls=%fused_computation | custom fusion | bytes 861280 | tf_op jit(solution)/shard_map/jit(_take)/gather | solution.py:127
  14.1 1.9 gather.11
  16.0 1.9 broadcast_select_fusion.1
  18.0 7.3 %all-to-all-start = ((bf16[8,35,768]{2,1,0:T(8,128)(2,1)}), bf16[8,35,768]{2,1,0:T(8,128)(2,1)}, u32[]{:S(2)}, u32[]{:S(2)}) async-start(bf16[8,35,768]{2,1,0:T(8,128)(2,1)} %broadcast_select_fusion.1), calls=%async_computation | async-start | bytes 983040 | tf_op jit(solution)/shard_map/all_to_all | solution.py:129
  25.3 2.7 %convolution_convert_fusion.2 = bf16[256,768]{1,0:T(8,128)(2,1)} fusion(bf16[768,768]{1,0:T(8,128)(2,1)} %param.21, bf16[1,1,1,256,768]{4,3,2,1,0:T(8,128)(2,1)} %param.18), kind=kOutput, calls=%fused_computation.52 | convolution fusion | flops 302186496 | bytes 1966080 | tf_op jit(solution)/shard_map/dot_general | solution.py:62
  31.3 8.7 %all-to-all-done = bf16[8,35,768]{2,1,0:T(8,128)(2,1)} async-done(((bf16[8,35,768]{2,1,0:T(8,128)(2,1)}), bf16[8,35,768]{2,1,0:T(8,128)(2,1)}, u32[]{:S(2)}, u32[]{:S(2)}) %all-to-all-start) | async-done | bytes 430112 | tf_op jit(solution)/shard_map/all_to_all | solution.py:129
  40.0 1.9 reshape.239
  41.9 3.2 %gather_fusion.1 = bf16[256,768]{1,0:T(8,128)(2,1)} fusion(bf16[280,768]{1,0:T(8,128)(2,1)} %reshape.239, s32[1024]{0:T(1024)S(1)} %pad_clamp_fusion), kind=kCustom, calls=%fused_computation.1 | custom fusion | bytes 787456 | tf_op jit(solution)/shard_map/jit(_take)/gather | solution.py:132
  47.7 2.6 %fusion.54 = f32[256,2304]{0,1:T(8,128)S(1)} fusion(bf16[768,2304]{1,0:T(8,128)(2,1)S(1)} %copy-done, f32[256]{0:T(256)S(1)} %add_rsqrt_fusion.1, f32[256]{0:T(256)S(1)} %broadcast_multiply_fusion.1, bf16[256,768]{1,0:T(8,128)(2,1)} %gather_fusion.1, pred[256]{0:T(512)(128)(4,1)S(1)} %compare_and_fusion.1), kind=kOutput, calls=%fused_computation.166 | convolution fusion | flops 906952704 | bytes 6293760 | tf_op jit(solution)/shard_map/dot_general | solution.py:37
  51.2 3.4 %fusion.13 = (f32[12,256]{1,0:T(8,128)S(1)}, f32[12,256,256]{1,2,0:T(8,128)S(1)}) fusion(f32[12]{0:T(128)S(1)} %copy-done.43, pred[256,256]{0,1:T(8,128)(4,1)S(1)} %copy-done.6, f32[256,3,12,64]{0,3,2,1:T(8,128)S(1)} %bitcast.104, f32[256,12]{0,1:T(8,128)S(1)} %get-tuple-element.66, f32[256,12]{0,1:T(8,128)S(1)} %get-tuple-element.65), kind=kOutput, calls=%fused_computation.31 | convolution fusion | flops 606729216 | bytes 4829696 | tf_op jit(solution)/shard_map/qhd,khd->hqk/dot_general | solution.py:49
  56.7 3.3 %convolution_bitcast_fusion.2 = f32[256,12,64]{0,2,1:T(8,128)S(1)} fusion(f32[12,256,256]{1,2,0:T(8,128)S(1)} %get-tuple-element.64, f32[12,256]{1,0:T(8,128)S(1)} %get-tuple-element.63, f32[12]{0:T(128)S(1)} %copy-done.43, f32[256,3,12,64]{0,3,2,1:T(8,128)S(1)} %bitcast.107, f32[256,12]{0,1:T(8,128)S(1)} %get-tuple-element.66, ...), kind=kOutput, calls=%fused_computation.45 | convolution fusion | flops 608894976 | bytes 7979520 | tf_op jit(solution)/shard_map/hqk,khd->qhd/dot_general | solution.py:76
  60.0 4.0 %convolution_bitcast_fusion.1 = f32[256,12,64]{0,2,1:T(8,128)S(1)} fusion(f32[12,256,256]{1,2,0:T(8,128)S(1)} %get-tuple-element.64, f32[12,256]{1,0:T(8,128)S(1)} %get-tuple-element.63, f32[12]{0:T(128)S(1)} %copy-done.43, f32[256,3,12,64]{0,3,2,1:T(8,128)S(1)} %bitcast.108, f32[256,12]{0,1:T(8,128)S(1)} %get-tuple-element.65, ...), kind=kOutput, calls=%fused_computation.44 | convolution fusion | flops 608894976 | bytes 7979520 | tf_op jit(solution)/shard_map/hqk,qhd->khd/dot_general | solution.py:77
  66.3 4.1 %fusion.52 = f32[2304,768]{1,0:T(8,128)} fusion(bf16[256,2304]{0,1:T(8,128)(2,1)S(1)} %bitcast.101, f32[256]{0:T(256)S(1)} %add_rsqrt_fusion.1, f32[256]{0:T(256)S(1)} %broadcast_multiply_fusion.1, bf16[256,768]{1,0:T(8,128)(2,1)S(1)} %copy-done.1, pred[256]{0:T(512)(128)(4,1)S(1)} %compare_and_fusion.1), kind=kOutput, calls=%fused_computation.165 | convolution fusion | flops 906952704 | bytes 8653056 | tf_op jit(solution)/shard_map/dot_general | solution.py:92
  70.4 1.9 convolution_bitcast_fusion
  72.3 8.0 %pad_maximum_fusion = f32[3072,768]{1,0:T(8,128)} fusion(f32[768,768]{1,0:T(8,128)} %convolution_bitcast_fusion, f32[2304,768]{1,0:T(8,128)} %fusion.52), kind=kLoop, calls=%fused_computation.7 | loop fusion | flops 2359296 | bytes 18874368 | tf_op jit(solution)/shard_map/concatenate | solution.py:90
  80.3 2.7 %fusion.21 = bf16[256,768]{1,0:T(8,128)(2,1)} fusion(bf16[256,768]{0,1:T(8,128)(2,1)} %bitcast.113, bf16[768,768]{1,0:T(8,128)(2,1)} %param.21, bf16[256,768]{1,0:T(8,128)(2,1)} %gather_fusion.1, pred[256]{0:T(512)(128)(4,1)S(1)} %compare_and_fusion.1), kind=kOutput, calls=%fused_computation.47 | convolution fusion | flops 302776320 | bytes 2359552 | tf_op jit(solution)/shard_map/dot_general | solution.py:60
  83.0 2.8 %scatter_custom_fusion.1 = bf16[280,768]{1,0:T(8,128)(2,1)} fusion(s32[256]{0:T(256)S(1)} %bitcast.120, bf16[256,768]{1,0:T(8,128)(2,1)} %fusion.21, bf16[]{:T(256)} %constant.23.clone.1), kind=kCustom, calls=%fused_computation.89 | custom fusion | bytes 430592 | tf_op jit(solution)/shard_map/scatter | solution.py:154
  85.9 1.9 reshape.244
  87.8 4.1 %all-to-all-start.1 = ((bf16[8,35,768]{2,1,0:T(8,128)(2,1)}), bf16[8,35,768]{2,1,0:T(8,128)(2,1)}, u32[]{:S(2)}, u32[]{:S(2)}) async-start(bf16[8,35,768]{2,1,0:T(8,128)(2,1)} %reshape.244), calls=%async_computation.2 | async-start | bytes 983040 | tf_op jit(solution)/shard_map/all_to_all | solution.py:156
  92.0 2.2 scatter_custom_fusion
  98.0 7.5 %all-to-all-done.1 = bf16[8,35,768]{2,1,0:T(8,128)(2,1)} async-done(((bf16[8,35,768]{2,1,0:T(8,128)(2,1)}), bf16[8,35,768]{2,1,0:T(8,128)(2,1)}, u32[]{:S(2)}, u32[]{:S(2)}) %all-to-all-start.1) | async-done | bytes 430112 | tf_op jit(solution)/shard_map/all_to_all | solution.py:156
  105.5 2.0 reshape.245
  107.5 2.3 convolution_convert_fusion.3
  109.8 2.9 %scatter_custom_fusion.2 = bf16[1024,384]{1,0:T(8,128)(2,1)} fusion(s32[280]{0:T(512)} %get-tuple-element.53, bf16[280,384]{1,0:T(8,128)(2,1)} %convolution_convert_fusion.3, bf16[]{:T(256)} %constant.23.clone.1), kind=kCustom, calls=%fused_computation.85 | custom fusion | bytes 786944 | tf_op jit(solution)/shard_map/scatter | solution.py:166
  119.8 3.8 %collective-permute-start.5 = (bf16[38,3,384]{2,1,0:T(4,128)(2,1)S(1)}, bf16[38,3,384]{2,1,0:T(4,128)(2,1)S(1)}, u32[]{:S(2)}, u32[]{:S(2)}) collective-permute-start(bf16[38,3,384]{2,1,0:T(4,128)(2,1)S(1)} %get-tuple-element.58), channel_id=1, source_target_pairs={{4,0},{8,4},{12,8},{0,12},{5,1},{9,5},{13,9},{1,13},{6,2},{10,6},{... | collective-permute-start | bytes 262664 | tf_op jit(solution)/shard_map/ppermute | solution.py:20
  123.7 2.8 %collective-permute-done.4 = bf16[38,3,384]{2,1,0:T(4,128)(2,1)S(1)} collective-permute-done((bf16[38,3,384]{2,1,0:T(4,128)(2,1)S(1)}, bf16[38,3,384]{2,1,0:T(4,128)(2,1)S(1)}, u32[]{:S(2)}, u32[]{:S(2)}) %collective-permute-start.4) | collective-permute-done | bytes 87584 | tf_op jit(solution)/shard_map/ppermute | solution.py:17
  127.3 11.6 %fusion.67 = (f32[32,32]{1,0:T(8,128)S(1)}, f32[32,32,384]{2,1,0:T(8,128)S(1)}) fusion(bf16[38,38,384]{2,1,0:T(8,128)(2,1)S(1)} %maximum_select_fusion, f32[384]{0:T(512)S(1)} %get-tuple-element.51, f32[384]{0:T(512)S(1)} %get-tuple-element.52, f32[384]{0:T(512)S(1)} %get-tuple-element.5, f32[384]{0:T(512)S(1)} %get-tuple-element.6, ...), kind=kLoop, calls=%fused_computation.168 | loop fusion | flops 57801728 | bytes 40187392 | tf_op jit(solution)/shard_map/reduce_sum | solution.py:26
  140.5 72.8 %reduce-scatter.2.cloned.1.call-done = f32[96,768]{1,0:T(8,128)} async-done(((f32[3072,768]{1,0:T(8,128)}), f32[96,768]{1,0:T(8,128)}) %reduce-scatter.2.cloned.1.call-update) | async-done | bytes 294928 | tf_op jit(solution)/shard_map/reduce_scatter | solution.py:136
  214.4 9.3 %fusion.4 = bf16[1024,768]{1,0:T(8,128)(2,1)} fusion(bf16[1024,384]{1,0:T(8,128)(2,1)} %bitcast.111, bf16[384,768]{1,0:T(8,128)(2,1)} %param.25), kind=kOutput, calls=%fused_computation.11 | convolution fusion | flops 655097856 | bytes 2949120 | tf_op jit(solution)/shard_map/dot_general | solution.py:191
  225.9 3.8 %fusion.20 = f32[1024,128]{1,0:T(8,128)} fusion(bf16[384,128]{1,0:T(8,128)(2,1)} %param.27, bf16[1024,384]{1,0:T(8,128)(2,1)} %copy-done.2, bf16[1024,768]{1,0:T(8,128)(2,1)} %fusion.4, bf16[768,384]{1,0:T(8,128)(2,1)} %param.26), kind=kOutput, calls=%fused_computation.46 | convolution fusion | flops 705822720 | bytes 3571712 | tf_op jit(solution)/shard_map/dot_general | solution.py:197
  229.7 4.5 %collective-permute-done.1 = bf16[192,768]{1,0:T(8,128)(2,1)} collective-permute-done((bf16[192,768]{1,0:T(8,128)(2,1)}, bf16[192,768]{1,0:T(8,128)(2,1)}, u32[]{:S(2)}, u32[]{:S(2)}) %collective-permute-start.1) | collective-permute-done | bytes 294944 | tf_op jit(solution)/shard_map/ppermute | solution.py:143
  234.1 2.4 fusion.37
  (135 shorter events, 29.8 us)
Async XLA Ops:
  7.2 40.5 %copy-start = (bf16[768,2304]{1,0:T(8,128)(2,1)S(1)}, bf16[768,2304]{1,0:T(8,128)(2,1)}, u32[]{:S(2)}) copy-start(bf16[768,2304]{1,0:T(8,128)(2,1)} %param.19) | copy-start | bytes 10616836
  18.0 22.0 %all-to-all-start = ((bf16[8,35,768]{2,1,0:T(8,128)(2,1)}), bf16[8,35,768]{2,1,0:T(8,128)(2,1)}, u32[]{:S(2)}, u32[]{:S(2)}) async-start(bf16[8,35,768]{2,1,0:T(8,128)(2,1)} %broadcast_select_fusion.1), calls=%async_computation | async-start | bytes 983040 | tf_op jit(solution)/shard_map/all_to_all | solution.py:129
  25.2 188.1 %reduce-scatter.2.cloned.1.call-start = ((), (), s32[]{:S(2)}) async-start(), calls=%async_computation.3 | async-start | bytes 9732096 | tf_op jit(solution)/shard_map/reduce_scatter | solution.py:136
  55.4 15.0 %copy-start.4 = (bf16[12,64,256]{2,1,0:T(8,128)(2,1)}, bf16[12,64,256]{2,1,0:T(8,128)(2,1)S(1)}, u32[]{:S(2)}) copy-start(bf16[12,64,256]{2,1,0:T(8,128)(2,1)S(1)} %convolution_convert_fusion) | copy-start | bytes 1179652
  87.8 17.7 %all-to-all-start.1 = ((bf16[8,35,768]{2,1,0:T(8,128)(2,1)}), bf16[8,35,768]{2,1,0:T(8,128)(2,1)}, u32[]{:S(2)}, u32[]{:S(2)}) async-start(bf16[8,35,768]{2,1,0:T(8,128)(2,1)} %reshape.244), calls=%async_computation.2 | async-start | bytes 983040 | tf_op jit(solution)/shard_map/all_to_all | solution.py:156
  114.1 12.8 %copy-start.2 = (bf16[1024,384]{1,0:T(8,128)(2,1)}, bf16[1024,384]{1,0:T(8,128)(2,1)S(1)}, u32[]{:S(2)}) copy-start(bf16[1024,384]{1,0:T(8,128)(2,1)S(1)} %broadcast_select_fusion) | copy-start | bytes 2359300
  114.2 4.4 %collective-permute-start.2 = (bf16[3,32,384]{2,1,0:T(8,128)(2,1)S(1)}, bf16[3,32,384]{2,1,0:T(8,128)(2,1)S(1)}, u32[]{:S(2)}, u32[]{:S(2)}) collective-permute-start(bf16[3,32,384]{2,1,0:T(8,128)(2,1)S(1)} %bitcast.117), channel_id=1, source_target_pairs={{0,16},{16,0},{1,17},{17,1},{2,18},{18,2},{3,19},{19,3},{4,20},{20... | collective-permute-start | bytes 221192 | tf_op jit(solution)/shard_map/ppermute | solution.py:17
  114.8 4.6 %collective-permute-start.3 = (bf16[3,32,384]{2,1,0:T(8,128)(2,1)S(1)}, bf16[3,32,384]{2,1,0:T(8,128)(2,1)S(1)}, u32[]{:S(2)}, u32[]{:S(2)}) collective-permute-start(bf16[3,32,384]{2,1,0:T(8,128)(2,1)S(1)} %bitcast.116), channel_id=1, source_target_pairs={{16,0},{0,16},{17,1},{1,17},{18,2},{2,18},{19,3},{3,19},{20,4},{4,... | collective-permute-start | bytes 221192 | tf_op jit(solution)/shard_map/ppermute | solution.py:20
  119.4 7.6 %copy-start.11 = (f32[384]{0:T(512)S(1)}, f32[384]{0:T(512)}, u32[]{:S(2)}) copy-start(f32[384]{0:T(512)} %get-tuple-element.12) | copy-start | bytes 4612
  119.4 7.6 %copy-start.12 = (f32[384]{0:T(512)S(1)}, f32[384]{0:T(512)}, u32[]{:S(2)}) copy-start(f32[384]{0:T(512)} %get-tuple-element.13) | copy-start | bytes 4612
  119.4 7.6 %copy-start.13 = (f32[384]{0:T(512)S(1)}, f32[384]{0:T(512)}, u32[]{:S(2)}) copy-start(f32[384]{0:T(512)} %get-tuple-element.14) | copy-start | bytes 4612
  119.4 7.6 %copy-start.14 = (f32[384]{0:T(512)S(1)}, f32[384]{0:T(512)}, u32[]{:S(2)}) copy-start(f32[384]{0:T(512)} %get-tuple-element.15) | copy-start | bytes 4612
  119.4 7.6 %copy-start.15 = (f32[384]{0:T(512)S(1)}, f32[384]{0:T(512)}, u32[]{:S(2)}) copy-start(f32[384]{0:T(512)} %get-tuple-element.16) | copy-start | bytes 4612
  119.4 7.6 %copy-start.16 = (f32[384]{0:T(512)S(1)}, f32[384]{0:T(512)}, u32[]{:S(2)}) copy-start(f32[384]{0:T(512)} %get-tuple-element.17) | copy-start | bytes 4612
  119.4 7.6 %copy-start.17 = (f32[384]{0:T(512)S(1)}, f32[384]{0:T(512)}, u32[]{:S(2)}) copy-start(f32[384]{0:T(512)} %get-tuple-element.18) | copy-start | bytes 4612
  119.5 7.6 %copy-start.18 = (f32[384]{0:T(512)S(1)}, f32[384]{0:T(512)}, u32[]{:S(2)}) copy-start(f32[384]{0:T(512)} %get-tuple-element.19) | copy-start | bytes 4612
  119.5 7.6 %copy-start.19 = (f32[384]{0:T(512)S(1)}, f32[384]{0:T(512)}, u32[]{:S(2)}) copy-start(f32[384]{0:T(512)} %get-tuple-element.20) | copy-start | bytes 4612
  119.5 7.6 %copy-start.20 = (f32[384]{0:T(512)S(1)}, f32[384]{0:T(512)}, u32[]{:S(2)}) copy-start(f32[384]{0:T(512)} %get-tuple-element.21) | copy-start | bytes 4612
  119.5 7.6 %copy-start.21 = (f32[384]{0:T(512)S(1)}, f32[384]{0:T(512)}, u32[]{:S(2)}) copy-start(f32[384]{0:T(512)} %get-tuple-element.22) | copy-start | bytes 4612
  119.5 7.6 %copy-start.22 = (f32[384]{0:T(512)S(1)}, f32[384]{0:T(512)}, u32[]{:S(2)}) copy-start(f32[384]{0:T(512)} %get-tuple-element.23) | copy-start | bytes 4612
  119.5 7.6 %copy-start.23 = (f32[384]{0:T(512)S(1)}, f32[384]{0:T(512)}, u32[]{:S(2)}) copy-start(f32[384]{0:T(512)} %get-tuple-element.24) | copy-start | bytes 4612
  119.5 7.6 %copy-start.24 = (f32[384]{0:T(512)S(1)}, f32[384]{0:T(512)}, u32[]{:S(2)}) copy-start(f32[384]{0:T(512)} %get-tuple-element.25) | copy-start | bytes 4612
  119.5 7.6 %copy-start.25 = (f32[384]{0:T(512)S(1)}, f32[384]{0:T(512)}, u32[]{:S(2)}) copy-start(f32[384]{0:T(512)} %get-tuple-element.26) | copy-start | bytes 4612
  119.5 7.6 %copy-start.26 = (f32[384]{0:T(512)S(1)}, f32[384]{0:T(512)}, u32[]{:S(2)}) copy-start(f32[384]{0:T(512)} %get-tuple-element.27) | copy-start | bytes 4612
  119.5 7.6 %copy-start.27 = (f32[384]{0:T(512)S(1)}, f32[384]{0:T(512)}, u32[]{:S(2)}) copy-start(f32[384]{0:T(512)} %get-tuple-element.28) | copy-start | bytes 4612
  119.5 7.6 %copy-start.28 = (f32[384]{0:T(512)S(1)}, f32[384]{0:T(512)}, u32[]{:S(2)}) copy-start(f32[384]{0:T(512)} %get-tuple-element.29) | copy-start | bytes 4612
  119.6 7.6 %copy-start.29 = (f32[384]{0:T(512)S(1)}, f32[384]{0:T(512)}, u32[]{:S(2)}) copy-start(f32[384]{0:T(512)} %get-tuple-element.30) | copy-start | bytes 4612
  119.6 7.6 %copy-start.30 = (f32[384]{0:T(512)S(1)}, f32[384]{0:T(512)}, u32[]{:S(2)}) copy-start(f32[384]{0:T(512)} %get-tuple-element.31) | copy-start | bytes 4612
  119.8 6.7 %collective-permute-start.4 = (bf16[38,3,384]{2,1,0:T(4,128)(2,1)S(1)}, bf16[38,3,384]{2,1,0:T(4,128)(2,1)S(1)}, u32[]{:S(2)}, u32[]{:S(2)}) collective-permute-start(bf16[38,3,384]{2,1,0:T(4,128)(2,1)S(1)} %get-tuple-element.57), channel_id=1, source_target_pairs={{0,4},{4,8},{8,12},{12,0},{1,5},{5,9},{9,13},{13,1},{2,6},{6,10},{... | collective-permute-start | bytes 262664 | tf_op jit(solution)/shard_map/ppermute | solution.py:17
  119.8 6.6 %collective-permute-start.5 = (bf16[38,3,384]{2,1,0:T(4,128)(2,1)S(1)}, bf16[38,3,384]{2,1,0:T(4,128)(2,1)S(1)}, u32[]{:S(2)}, u32[]{:S(2)}) collective-permute-start(bf16[38,3,384]{2,1,0:T(4,128)(2,1)S(1)} %get-tuple-element.58), channel_id=1, source_target_pairs={{4,0},{8,4},{12,8},{0,12},{5,1},{9,5},{13,9},{1,13},{6,2},{10,6},{... | collective-permute-start | bytes 262664 | tf_op jit(solution)/shard_map/ppermute | solution.py:20
  214.3 9.3 %collective-permute-start = (bf16[96,768]{1,0:T(8,128)(2,1)S(1)}, bf16[96,768]{1,0:T(8,128)(2,1)S(1)}, u32[]{:S(2)}, u32[]{:S(2)}) collective-permute-start(bf16[96,768]{1,0:T(8,128)(2,1)S(1)} %convert_element_type.212), channel_id=1, source_target_pairs={{0,1},{1,0},{2,3},{3,2},{4,5},{5,4},{6,7},{7,6},{8,9},{9,8},{10,11... | collective-permute-start | bytes 442376 | tf_op jit(solution)/shard_map/ppermute | solution.py:143
  224.4 9.7 %collective-permute-start.1 = (bf16[192,768]{1,0:T(8,128)(2,1)}, bf16[192,768]{1,0:T(8,128)(2,1)}, u32[]{:S(2)}, u32[]{:S(2)}) collective-permute-start(bf16[192,768]{1,0:T(8,128)(2,1)} %maximum_select_fusion.2), channel_id=1, source_target_pairs={{0,2},{1,3},{2,0},{3,1},{4,6},{5,7},{6,4},{7,5},{8,10},{9,11},{10,... | collective-permute-start | bytes 884744 | tf_op jit(solution)/shard_map/ppermute | solution.py:143
  (21 other events, 124.1 us)
Sparse Core Ops, SparseCore 0:
  80.4 132.8 reduce-scatter.1
